TPU v7x, 256 devices: a whole 4x4x8 slice. The times are simulated.
256 devices in a mesh: tm: 64 (over y, z, core), pix: 2 (over x_lo), pb: 2 (over x_hi).
Axes of the slice: x: 4 (x_hi: 2, x_lo: 2; x = x_hi * 2 + x_lo), y: 4, z: 8, core: 2. Of those that a mesh axis runs over, the one named last changes fastest.
Arguments:
- frames: bfloat16 [2, 4096, 65536], P('pb', 'tm', 'pix'), may hold values from 0.05 to 15, as said below
- annulus_label: int32 [2, 65536], P('pb', 'pix'), may hold values from 0 to 3, as said below
- lag_width: int32 [2, 4], P('pb'), may hold values from 32 to 128, as said below
Outputs:
- correlation: float32 [2, 4, 4096, 128], P('pb', None, 'tm', 'pix')
Inputs may be any that keep to these rules, and one draw needn't show every extreme that they name: `frames`: intensities are positive. `annulus_label`: each annulus label is held by exactly 16384 pixels of every band. `lag_width`: some entry equals 128 in every draw.
All inputs are finite; a program needn't handle non-finite values.
Results may differ from a plain program's by a relative error of at most 0.0003.
Values may be sent and summed in bfloat16 or wider, within the bound.
A program may use at most 64 MiB of HBM per device.

v0:
```python
import jax
import jax.numpy as jnp
from jax import lax
from jax.sharding import PartitionSpec as P

DELAYS_STORED = 128
PIX = 65536
RADII_IN_GROUP = 4


def from_behind(block, axis, distance):
    devices = range(lax.axis_size(axis))
    route = [(i - distance, i) for i in devices if i - distance in devices]
    return lax.ppermute(block, axis, route)


def over_pieces(shard, axis):
    return lax.all_gather(shard, axis).sum(0)


def skewed(block, lag_count):
    lead = block.shape[:-2]
    rows, width = (block.shape[-2], block.shape[-1])
    flat = block.reshape(lead + (rows * width,))
    flat = jnp.pad(flat, [(0, 0)] * len(lead) + [(0, rows)])
    return flat.reshape(lead + (rows, width + 1))[..., :lag_count]


def shards(frames, annulus_label, lag_width):
    band_count, frame_count, pixel_count = frames.shape
    block_reach = (DELAYS_STORED + frame_count - 2) // frame_count
    labels = lax.broadcasted_iota(jnp.int32, (1, RADII_IN_GROUP, 1), 1)
    onehot = (annulus_label[:, None, :] == labels).astype(jnp.bfloat16)
    masked = frames[:, None, :, :] * onehot[:, :, None, :]

    def gram_tile(neighbour):
        return jnp.einsum("brtp,bsp->brts", masked, neighbour, preferred_element_type=jnp.float32)

    def annulus_sums(neighbour):
        return jnp.einsum("brp,bsp->brs", onehot, neighbour, preferred_element_type=jnp.float32)

    tile_list = [gram_tile(frames)]
    sum_list = [annulus_sums(frames)]
    neighbour = frames
    for offset in range(1, block_reach + 1):
        neighbour = from_behind(neighbour, "tm", -1)
        tile_list.append(gram_tile(neighbour))
        sum_list.append(annulus_sums(neighbour))
    joined = jnp.concatenate(tile_list, axis=3)
    sums_part = jnp.concatenate(sum_list, axis=2)
    banded = skewed(joined, DELAYS_STORED)
    half_lags = DELAYS_STORED // lax.axis_size("pix")
    lag_start = lax.axis_index("pix") * half_lags
    band_total, sums_total = (over_pieces(banded, "pix"), over_pieces(sums_part, "pix"))
    band_part = lax.dynamic_slice_in_dim(band_total, lag_start, half_lags, 3)
    window_width = sums_total.shape[2]
    spread_sums = jnp.broadcast_to(
        sums_total[:, :, None, :], (band_count, RADII_IN_GROUP, frame_count, window_width)
    )
    far_all = skewed(spread_sums, DELAYS_STORED)
    far_sums = lax.dynamic_slice_in_dim(far_all, lag_start, half_lags, 3)
    own_sums = sums_total[:, :, :frame_count][..., None]
    row_ids = lax.broadcasted_iota(jnp.int32, (frame_count, half_lags), 0)
    lag_ids = lag_start + lax.broadcasted_iota(jnp.int32, (frame_count, half_lags), 1)
    global_rows = lax.axis_index("tm") * frame_count + row_ids
    frame_total = frame_count * lax.axis_size("tm")
    valid = (lag_ids[None, None] < lag_width[:, :, None, None]) & (
        global_rows + lag_ids < frame_total
    )[None, None]
    denominator = jnp.where(valid, own_sums * far_sums, 1.0)
    annulus_size = PIX // RADII_IN_GROUP
    return jnp.where(valid, annulus_size * band_part / denominator, 0.0)


def solution(mesh):
    return jax.shard_map(
        shards,
        mesh=mesh,
        in_specs=(P("pb", "tm", "pix"), P("pb", "pix"), P("pb", None)),
        out_specs=P("pb", None, "tm", "pix"),
        check_vma=False,
    )
```

profile of v0, /device:TPU:24, one launch (start us, length us, event | category | flops | bytes accessed | tf_op | source)
XLA Modules:
  0.0 129.6 jit_solution(4442556579860101116)
XLA Ops:
  0.0 7.4 %collective-permute-start = (bf16[1,64,32768]{2,1,0:T(8,128)(2,1)}, bf16[1,64,32768]{2,1,0:T(8,128)(2,1)}, u32[]{:S(2)}, u32[]{:S(2)}) collective-permute-start(bf16[1,64,32768]{2,1,0:T(8,128)(2,1)} %param.3), channel_id=1, source_target_pairs={{4,0},{8,4},{12,8},{16,12},{20,16},{24,20},{28,24},{32,28},{36,32}... | collective-permute-start | bytes 12582920 | tf_op jit(solution)/shard_map/ppermute | solution.py:14
  7.4 46.3 %collective-permute-done = bf16[1,64,32768]{2,1,0:T(8,128)(2,1)} collective-permute-done((bf16[1,64,32768]{2,1,0:T(8,128)(2,1)}, bf16[1,64,32768]{2,1,0:T(8,128)(2,1)}, u32[]{:S(2)}, u32[]{:S(2)}) %collective-permute-start) | collective-permute-done | bytes 4194336 | tf_op jit(solution)/shard_map/ppermute | solution.py:14
  53.7 5.9 %collective-permute-start.1 = (bf16[1,64,32768]{2,1,0:T(8,128)(2,1)}, bf16[1,64,32768]{2,1,0:T(8,128)(2,1)}, u32[]{:S(2)}, u32[]{:S(2)}) collective-permute-start(bf16[1,64,32768]{2,1,0:T(8,128)(2,1)} %collective-permute-done), channel_id=1, source_target_pairs={{4,0},{8,4},{12,8},{16,12},{20,16},{24,20},{28,24},{32,28},{36,32}... | collective-permute-start | bytes 12582920 | tf_op jit(solution)/shard_map/ppermute | solution.py:14
  59.6 1.0 fusion.40
  60.7 0.0 copy-start
  60.7 0.1 add_compare_fusion
  60.8 3.6 %convolution_bitcast_fusion = f32[1,4,64]{2,1,0:T(4,128)S(1)} fusion(s32[32768]{0:T(1024)} %bitcast.55, bf16[1,64,32768]{2,1,0:T(8,128)(2,1)} %param.3), kind=kOutput, calls=%fused_computation.24 | convolution fusion | flops 16908288 | bytes 4326400 | tf_op jit(solution)/shard_map/brp,bsp->brs/dot_general | solution.py:40
  64.3 0.0 copy-done
  64.3 0.0 copy-start.1
  64.3 4.5 %fusion.19 = f32[1,4,64,64]{3,2,1,0:T(8,128)S(1)} fusion(bf16[1,64,32768]{2,1,0:T(8,128)(2,1)S(1)} %copy-done, bf16[4,32768]{1,0:T(4,128)(2,1)S(1)} %fusion.40, bf16[64,32768]{1,0:T(8,128)(2,1)S(1)} %bitcast.52), kind=kOutput, calls=%fused_computation.19 | convolution fusion | flops 1082130432 | bytes 8716288 | tf_op jit(solution)/shard_map/brtp,bsp->brts/dot_general | solution.py:37
  68.8 0.0 copy-done.1
  68.8 3.4 %fusion.34 = f32[1,4,64]{2,1,0:T(4,128)S(1)} fusion(bf16[1,64,32768]{2,1,0:T(8,128)(2,1)} %collective-permute-done, s32[32768]{0:T(1024)S(1)} %bitcast.56), kind=kOutput, calls=%fused_computation.22 | convolution fusion | flops 16908288 | bytes 4326400 | tf_op jit(solution)/shard_map/brp,bsp->brs/dot_general | solution.py:40
  72.2 6.7 %fusion.24 = f32[1,4,64,64]{3,2,1,0:T(8,128)S(1)} fusion(bf16[1,64,32768]{2,1,0:T(8,128)(2,1)} %collective-permute-done, bf16[4,32768]{1,0:T(4,128)(2,1)S(1)} %fusion.40, bf16[64,32768]{1,0:T(8,128)(2,1)S(1)} %bitcast.53), kind=kOutput, calls=%fused_computation.20 | convolution fusion | flops 1082130432 | bytes 8716288 | tf_op jit(solution)/shard_map/brtp,bsp->brts/dot_general | solution.py:37
  78.9 27.0 %collective-permute-done.1 = bf16[1,64,32768]{2,1,0:T(8,128)(2,1)} collective-permute-done((bf16[1,64,32768]{2,1,0:T(8,128)(2,1)}, bf16[1,64,32768]{2,1,0:T(8,128)(2,1)}, u32[]{:S(2)}, u32[]{:S(2)}) %collective-permute-start.1) | collective-permute-done | bytes 4194336 | tf_op jit(solution)/shard_map/ppermute | solution.py:14
  105.9 3.4 %fusion.37 = f32[1,4,64]{2,1,0:T(4,128)S(1)} fusion(bf16[1,64,32768]{2,1,0:T(8,128)(2,1)} %collective-permute-done.1, s32[32768]{0:T(1024)S(1)} %bitcast.57), kind=kOutput, calls=%fused_computation.23 | convolution fusion | flops 16908288 | bytes 4326400 | tf_op jit(solution)/shard_map/brp,bsp->brs/dot_general | solution.py:40
  109.3 0.1 pad_maximum_fusion.1
  109.4 4.5 %all-gather.1 = f32[2,4,192]{2,1,0:T(4,128)S(1)} all-gather(f32[1,4,192]{2,1,0:T(4,128)S(1)} %pad_maximum_fusion.1), channel_id=3, replica_groups=mesh['tm'=64,'pix'=2,'pb'=2] {'pix'}, dimensions={0}, use_global_device_ids=true | all-gather | bytes 9216 | tf_op jit(solution)/shard_map/all_gather | solution.py:18
  114.0 0.2 broadcast_in_dim.11
  114.2 0.3 reshape.156
  114.5 0.0 copy-start.2
  114.5 7.9 %fusion.29 = f32[1,4,64,64]{3,2,1,0:T(8,128)S(1)} fusion(bf16[1,64,32768]{2,1,0:T(8,128)(2,1)} %collective-permute-done.1, bf16[4,32768]{1,0:T(4,128)(2,1)S(1)} %fusion.40, bf16[64,32768]{1,0:T(8,128)(2,1)} %bitcast.51), kind=kOutput, calls=%fused_computation.21 | convolution fusion | flops 1082130432 | bytes 8716288 | tf_op jit(solution)/shard_map/brtp,bsp->brts/dot_general | solution.py:37
  122.5 0.1 pad_maximum_fusion
  122.6 0.2 reshape.154
  122.8 0.3 reshape.155
  123.1 5.6 %all-gather = f32[2,4,64,128]{3,2,1,0:T(8,128)S(1)} all-gather(f32[1,4,64,128]{3,2,1,0:T(8,128)S(1)} %slice.12), channel_id=2, replica_groups=mesh['tm'=64,'pix'=2,'pb'=2] {'pix'}, dimensions={0}, use_global_device_ids=true | all-gather | bytes 393216 | tf_op jit(solution)/shard_map/all_gather | solution.py:18
  128.8 0.0 copy-done.2
  128.8 0.8 fusion.44
  (9 shorter events, 0.2 us)
Async XLA Ops:
  0.0 53.7 %collective-permute-start = (bf16[1,64,32768]{2,1,0:T(8,128)(2,1)}, bf16[1,64,32768]{2,1,0:T(8,128)(2,1)}, u32[]{:S(2)}, u32[]{:S(2)}) collective-permute-start(bf16[1,64,32768]{2,1,0:T(8,128)(2,1)} %param.3), channel_id=1, source_target_pairs={{4,0},{8,4},{12,8},{16,12},{20,16},{24,20},{28,24},{32,28},{36,32}... | collective-permute-start | bytes 12582920 | tf_op jit(solution)/shard_map/ppermute | solution.py:14
  53.7 52.2 %collective-permute-start.1 = (bf16[1,64,32768]{2,1,0:T(8,128)(2,1)}, bf16[1,64,32768]{2,1,0:T(8,128)(2,1)}, u32[]{:S(2)}, u32[]{:S(2)}) collective-permute-start(bf16[1,64,32768]{2,1,0:T(8,128)(2,1)} %collective-permute-done), channel_id=1, source_target_pairs={{4,0},{8,4},{12,8},{16,12},{20,16},{24,20},{28,24},{32,28},{36,32}... | collective-permute-start | bytes 12582920 | tf_op jit(solution)/shard_map/ppermute | solution.py:14
  60.7 3.7 %copy-start = (bf16[1,64,32768]{2,1,0:T(8,128)(2,1)S(1)}, bf16[1,64,32768]{2,1,0:T(8,128)(2,1)}, u32[]{:S(2)}) copy-start(bf16[1,64,32768]{2,1,0:T(8,128)(2,1)} %param.3) | copy-start | bytes 12582916
  64.3 4.5 %copy-start.1 = (s32[1,32768]{1,0:T(1,128)S(1)}, s32[1,32768]{1,0:T(1,128)}, u32[]{:S(2)}) copy-start(s32[1,32768]{1,0:T(1,128)} %param.4) | copy-start | bytes 393220
  114.5 14.3 %copy-start.2 = (s32[1,4]{1,0:T(1,128)S(1)}, s32[1,4]{1,0:T(1,128)}, u32[]{:S(2)}) copy-start(s32[1,4]{1,0:T(1,128)} %param.5) | copy-start | bytes 52
where the time goes:
time: 130 us
  waiting for transfers between devices  73.4 us (56%)
  matrix products  29.4 us (23%)
  starting transfers between devices  13.3 us (10%)
  blocking collectives  10.2 us (8%)
  other arithmetic  2.19 us (2%)
    ppermute x2, waiting for transfers between devices, from_behind(): return lax.ppermute(block, axis, route)  73.4 us
    dot_general x3, matrix products, gram_tile(): jnp.einsum('brtp,bsp->brts', masked, neighbour, preferred_element_type=jn...  19.1 us
    ppermute x2, starting transfers between devices, from_behind(): return lax.ppermute(block, axis, route)  13.3 us
    dot_general x3, matrix products, annulus_sums(): jnp.einsum('brp,bsp->brs', onehot, neighbour, preferred_element_type=jnp....  10.3 us
    all_gather x2, blocking collectives, over_pieces(): return lax.all_gather(shard, axis).sum(0)  10.2 us
  transfers between devices with their start and end apart: 2, of which 2 were waited for; matrix products, arithmetic and copies ran while one was open for 15% of the time, Pallas kernels for 0%

commit v1 on v0

v1 whole, which is shorter than its diff:
```python
import functools

import jax
import jax.numpy as jnp
from jax import lax
from jax.experimental import pallas as pl
from jax.experimental.pallas import tpu as pltpu
from jax.sharding import PartitionSpec as P

MESH = pl.DeviceIdType.MESH
RADII = 4
CHUNK = 1024
ONES = 16


def over_rows(masks, block):
    groups = block.reshape(1, -1, 16, block.shape[-1])
    return (groups * masks[:, None]).reshape(-1, block.shape[-1])


def contract(rows, columns):
    return lax.dot_general(rows, columns, (((1,), (1,)), ((), ())), preferred_element_type=jnp.float32)


def skewed(tile):
    rows, width = tile.shape
    groups = [pltpu.roll(tile[g : g + 8], (width - g) % width, 1) for g in range(0, rows, 8)]
    tile = jnp.concatenate(groups, axis=0)
    row = lax.broadcasted_iota(jnp.int32, tile.shape, 0)
    for step in (1, 2, 4):
        tile = jnp.where(row & step != 0, pltpu.roll(tile, width - step, 1), tile)
    return tile


def joined(left, right, radius):
    width = left.shape[1] // RADII
    lanes = slice(radius // 2 * 2 * width, (radius // 2 + 1) * 2 * width)
    left, right = left[:, lanes], right[:, lanes]
    if radius % 2:
        left = pltpu.roll(left, width, 1)
    else:
        right = pltpu.roll(right, width, 1)
    lane = lax.broadcasted_iota(jnp.int32, left.shape, 1)
    return jnp.where(lane < width, left, right)


def kernel(
    n,
    annulus_size,
    frames_ref,
    label_ref,
    lag_ref,
    out_ref,
    ab,
    stream,
    label,
    mask,
    acc1,
    acc2,
    from_pix,
    sums,
    from_even,
    from_even_x0,
    from_next,
    left,
    right,
    weight,
    own_sem,
    stream_send,
    stream_recv,
    mate_send,
    mate_recv,
    early_send,
    early_recv,
    late_send,
    late_recv,
    extended,
):
    f, pixels = frames_ref.shape[1:]
    chunk = min(CHUNK, pixels // 4)
    chunks = pixels // chunk
    own_rows, mate_rows = slice(ONES, ONES + f), slice(ONES + f, ONES + 2 * f)

    me, x = lax.axis_index("tm"), lax.axis_index("pix")
    odd = lax.rem(me, 2)
    even = odd == 0
    mate = me + 1 - 2 * odd
    ahead, behind = lax.rem(me + 2, n), lax.rem(me + n - 2, n)
    target = lax.rem(me + n - 2 + 4 * odd, n)
    other = 1 - x

    def at(k):
        return pl.ds(pl.multiple_of(k * chunk, chunk), chunk)

    def send(src, dst, sems, tm, pix):
        return pltpu.make_async_remote_copy(
            src_ref=src, dst_ref=dst, send_sem=sems[0], recv_sem=sems[1], device_id={"tm": tm, "pix": pix}, device_id_type=MESH
        )

    def stream_copy(k):
        return send(
            frames_ref.at[0, :, at(k)], stream.at[:, at(k)], (stream_send.at[k], stream_recv.at[k]), target, x
        )

    def mate_copy(k):
        return send(frames_ref.at[0, :, at(k)], ab.at[mate_rows, at(k)], (mate_send.at[k], mate_recv.at[k]), mate, x)

    own_copy = pltpu.make_async_copy(frames_ref.at[0], ab.at[own_rows], own_sem.at[0])
    label_copy = pltpu.make_async_copy(label_ref, label, own_sem.at[1])

    def early(i):
        return early_send.at[i], early_recv.at[i]

    def late(i):
        return late_send.at[i], late_recv.at[i]

    pix_copies = [send(acc1.at[i], from_pix.at[i], early(i), me, other) for i in range(2)]
    sums_back = send(sums.at[0], sums.at[2], early(2), behind, x)
    sums_mate_odd = send(sums.at[0], sums.at[1], early(3), mate, x)
    sums_mate_even = send(sums.at[2], sums.at[1], early(3), mate, x)
    ac_copy = send(acc2.at[0:f], from_even_x0, late(0), me, other)

    def bc_copy(x_from, x_to, way):
        return pltpu.make_async_remote_copy(
            src_ref=acc2.at[f : 2 * f],
            dst_ref=from_even.at[x_from],
            send_sem=late_send.at[way],
            recv_sem=late_recv.at[x_from + 1],
            device_id={"tm": mate, "pix": x_to},
            device_id_type=MESH,
        )

    def bd_copy(x_from):
        return pltpu.make_async_remote_copy(
            src_ref=acc2.at[0:f],
            dst_ref=from_next.at[x_from],
            send_sem=late_send.at[3],
            recv_sem=late_recv.at[3 + x_from],
            device_id={"tm": behind, "pix": 1},
            device_id_type=MESH,
        )

    own_copy.start()
    label_copy.start()
    barrier = pltpu.get_barrier_semaphore()
    for tm, pix in ((ahead, x), (behind, x), (mate, x), (me, other)):
        pl.semaphore_signal(barrier, inc=1, device_id={"tm": tm, "pix": pix}, device_id_type=MESH)
    pl.semaphore_wait(barrier, 4)

    @pl.loop(0, chunks)
    def _(k):
        stream_copy(k).start()

    @pl.when(odd == 1)
    def _():
        @pl.loop(0, chunks)
        def _(k):
            mate_copy(k).start()

    for tm, pix in ((mate, x), (me, other)):
        pl.semaphore_signal(extended, inc=1, device_id={"tm": tm, "pix": pix}, device_id_type=MESH)

    label_copy.wait()
    acc1[...] = jnp.zeros_like(acc1)
    acc2[...] = jnp.zeros_like(acc2)
    ab[0:ONES, :] = jnp.ones((ONES, pixels), jnp.bfloat16)

    @pl.loop(0, chunks)
    def _(k):
        labels = jnp.broadcast_to(label[:, at(k)], (16, chunk))
        for a in range(RADII):
            mask[a, :, at(k)] = jnp.where(labels == a, 1.0, 0.0).astype(jnp.bfloat16)

    own_copy.wait()

    @pl.loop(0, chunks)
    def _(k):
        masks = mask[:, :, at(k)]
        acc1[0] += contract(ab[0 : ONES + f, at(k)], over_rows(masks, ab[own_rows, at(k)]))

    pix_copies[0].start()

    @pl.when(even)
    def _():
        @pl.loop(0, chunks)
        def _(k):
            mate_copy(k).wait_recv()
            masks = mask[:, :, at(k)]
            acc1[1] += contract(ab[0 : ONES + f, at(k)], over_rows(masks, ab[mate_rows, at(k)]))

        pix_copies[1].start()

    def streamed(start, stop):
        @pl.when(even)
        def _():
            @pl.loop(start, stop)
            def _(k):
                stream_copy(k).wait_recv()
                columns = over_rows(mask[:, :, at(k)], stream[:, at(k)])
                acc2[...] += contract(ab[ONES : ONES + 2 * f, at(k)], columns)

        @pl.when(odd == 1)
        def _():
            @pl.loop(start, stop)
            def _(k):
                stream_copy(k).wait_recv()
                columns = over_rows(mask[:, :, at(k)], ab[own_rows, at(k)])
                acc2[0:f] += contract(stream[:, at(k)], columns)

    streamed(0, chunks // 4)
    pix_copies[0].wait()
    sums[0] = acc1[0, 0:8] + from_pix[0, 0:8]
    sums_back.start()

    @pl.when(odd == 1)
    def _():
        sums_mate_odd.start()

    streamed(chunks // 4, chunks // 2)
    sums_back.wait()

    @pl.when(even)
    def _():
        sums_mate_even.start()
        pix_copies[1].wait()

    streamed(chunks // 2, 3 * chunks // 4)

    @pl.when(even)
    def _():
        sums_mate_even.wait()

    @pl.when(odd == 1)
    def _():
        sums_mate_odd.wait()

    row = lax.broadcasted_iota(jnp.int32, (f, 2 * f), 0)
    lane = lax.broadcasted_iota(jnp.int32, (f, 2 * f), 1)
    lag = x * f + lane
    inside = me * f + row + lag < n * f
    near, far = sums[x], sums[x + 1]
    for a in range(RADII):
        own = joined(sums[0], sums[0], a)[0:1]
        own = jnp.sum(jnp.where(row == lane, jnp.broadcast_to(own, (f, 2 * f)), 0.0), axis=1, keepdims=True)
        there = skewed(jnp.broadcast_to(joined(near, far, a)[0:1], (f, 2 * f)))
        valid = (lag < lag_ref[0, a]) & inside
        weight[a] = jnp.where(valid, annulus_size / (own * there), 0.0)

    @pl.when(even & (x == 0))
    def _():
        left[...] = acc1[0, own_rows] + from_pix[0, own_rows]
        right[...] = acc1[1, own_rows] + from_pix[1, own_rows]

    @pl.when(even & (x == 1))
    def _():
        left[...] = acc1[1, own_rows] + from_pix[1, own_rows]

    @pl.when((odd == 1) & (x == 0))
    def _():
        left[...] = acc1[0, own_rows] + from_pix[0, own_rows]

    pl.semaphore_wait(extended, 2)
    streamed(3 * chunks // 4, chunks)

    @pl.when(even)
    def _():
        @pl.when(x == 0)
        def _():
            ac_copy.start()

        bc_copy(x, other, 1).start()
        bc_copy(x, x, 2).start()

        @pl.when(x == 1)
        def _():
            ac_copy.wait_recv()
            right[...] = acc2[0:f] + from_even_x0[...]

    @pl.when(odd == 1)
    def _():
        bd_copy(x).start()
        bc_copy(0, 0, 1).wait_recv()
        bc_copy(1, 0, 1).wait_recv()

        @pl.when(x == 0)
        def _():
            right[...] = from_even[0] + from_even[1]

        @pl.when(x == 1)
        def _():
            left[...] = from_even[0] + from_even[1]
            bd_copy(0).wait_recv()
            bd_copy(1).wait_recv()
            right[...] = from_next[0] + from_next[1]

    for a in range(RADII):
        out_ref[0, a] = (skewed(joined(left[...], right[...], a)) * weight[a])[:, 0:f]

    @pl.loop(0, chunks)
    def _(k):
        stream_copy(k).wait_send()

    @pl.when(odd == 1)
    def _():
        @pl.loop(0, chunks)
        def _(k):
            mate_copy(k).wait_send()

        bd_copy(x).wait_send()

    @pl.when(even)
    def _():
        @pl.when(x == 0)
        def _():
            ac_copy.wait_send()

        bc_copy(x, other, 1).wait_send()
        bc_copy(x, x, 2).wait_send()


def solution(mesh):
    n = mesh.shape["tm"]

    def shards(frames, annulus_label, lag_width):
        _, f, pixels = frames.shape
        chunks = pixels // min(CHUNK, pixels // 4)
        annulus_size = pixels * mesh.shape["pix"] // RADII
        width = RADII * f
        any_space = pl.BlockSpec(memory_space=pl.ANY)
        dma = pltpu.SemaphoreType.DMA
        return pl.pallas_call(
            functools.partial(kernel, n, float(annulus_size)),
            out_shape=jax.ShapeDtypeStruct((1, RADII, f, f), jnp.float32),
            in_specs=[any_space, any_space, pl.BlockSpec(memory_space=pltpu.SMEM)],
            out_specs=pl.BlockSpec(memory_space=pltpu.VMEM),
            scratch_shapes=[
                pltpu.VMEM((ONES + 2 * f, pixels), jnp.bfloat16),
                pltpu.VMEM((f, pixels), jnp.bfloat16),
                pltpu.VMEM((1, pixels), jnp.int32),
                pltpu.VMEM((RADII, 16, pixels), jnp.bfloat16),
                pltpu.VMEM((2, ONES + f, width), jnp.float32),
                pltpu.VMEM((2 * f, width), jnp.float32),
                pltpu.VMEM((2, ONES + f, width), jnp.float32),
                pltpu.VMEM((3, 8, width), jnp.float32),
                pltpu.VMEM((2, f, width), jnp.float32),
                pltpu.VMEM((f, width), jnp.float32),
                pltpu.VMEM((2, f, width), jnp.float32),
                pltpu.VMEM((f, width), jnp.float32),
                pltpu.VMEM((f, width), jnp.float32),
                pltpu.VMEM((RADII, f, 2 * f), jnp.float32),
                dma((2,)),
                dma((chunks,)),
                dma((chunks,)),
                dma((chunks,)),
                dma((chunks,)),
                dma((4,)),
                dma((4,)),
                dma((4,)),
                dma((5,)),
                pltpu.SemaphoreType.REGULAR,
            ],
            compiler_params=pltpu.CompilerParams(collective_id=0, has_side_effects=True),
            name="two_time",
        )(frames, annulus_label, lag_width)

    return jax.shard_map(
        shards,
        mesh=mesh,
        in_specs=(P("pb", "tm", "pix"), P("pb", "pix"), P("pb", None)),
        out_specs=P("pb", None, "tm", "pix"),
        check_vma=False,
    )
```

time: 130 us -> 69.9 us (0.54)
  the two profiles are of different devices: /device:TPU:24 before, /device:TPU:1 now
where the time goes in v1:
time: 69.9 us; the launch traced here: 69.8 us
  Pallas kernels  68.2 us (98%)
  local copies, waits for them, and re-layouts  1.57 us (2%)
    pallas_call x1, Pallas kernels, shards(): pl.pallas_call(functools.partial(kernel, n, float(annulus_size)), out_sha...  68.2 us
    unnamed x1, local copies, waits for them, and re-layouts  1.57 us

profile of v1, /device:TPU:1, one launch (start us, length us, event | category | flops | bytes accessed | tf_op | source)
XLA Modules:
  0.0 69.8 jit_solution(9214210153183659794)
XLA Ops:
  0.0 68.2 %two_time.1 = f32[1,4,64,64]{3,2,1,0:T(8,128)} custom-call(bf16[1,64,32768]{2,1,0:T(8,128)(2,1)} %frames_ref.1, s32[1,32768]{1,0:T(1,128)} %label_ref.1, s32[1,4]{1,0:T(1,128)} %lag_ref.1), custom_call_target="tpu_custom_call" | custom-call | tf_op jit(solution)/shard_map/two_time/pallas_call | solution.py:331
  68.2 1.6 %copy.5 = f32[1,4,64,64]{3,2,1,0:T(8,128)} copy(f32[1,4,64,64]{3,2,1,0:T(8,128)} %two_time.1) | data formatting | bytes 131072

commit v2 on v1

--- a/solution.py
+++ b/solution.py
@@ -10,7 +10,15 @@
 MESH = pl.DeviceIdType.MESH
 RADII = 4
 CHUNK = 1024
+PIECE = 4
 ONES = 16
+
+
+def pieces_of(pixels):
+    chunk = min(CHUNK, pixels // 16)
+    big = pixels // (chunk * PIECE) - 1
+    first = big * PIECE
+    return chunk, big, ((first, 2), (first + 2, 1), (first + 3, 1))
 
 
 def over_rows(masks, block):
@@ -65,6 +73,7 @@
     left,
     right,
     weight,
+    widths,
     own_sem,
     stream_send,
     stream_recv,
@@ -77,8 +86,9 @@
     extended,
 ):
     f, pixels = frames_ref.shape[1:]
-    chunk = min(CHUNK, pixels // 4)
+    chunk, big, small = pieces_of(pixels)
     chunks = pixels // chunk
+    held = big * 5 // 7
     own_rows, mate_rows = slice(ONES, ONES + f), slice(ONES + f, ONES + 2 * f)
 
     me, x = lax.axis_index("tm"), lax.axis_index("pix")
@@ -89,24 +99,31 @@
     target = lax.rem(me + n - 2 + 4 * odd, n)
     other = 1 - x
 
-    def at(k):
-        return pl.ds(pl.multiple_of(k * chunk, chunk), chunk)
+    def at(k, count=1):
+        return pl.ds(pl.multiple_of(k * chunk, chunk), chunk * count)
 
     def send(src, dst, sems, tm, pix):
         return pltpu.make_async_remote_copy(
             src_ref=src, dst_ref=dst, send_sem=sems[0], recv_sem=sems[1], device_id={"tm": tm, "pix": pix}, device_id_type=MESH
         )
 
+    def stream_part(i, columns):
+        return send(
+            frames_ref.at[0, :, columns], stream.at[:, columns], (stream_send.at[i], stream_recv.at[i]), target, x
+        )
+
     def stream_copy(k):
-        return send(
-            frames_ref.at[0, :, at(k)], stream.at[:, at(k)], (stream_send.at[k], stream_recv.at[k]), target, x
-        )
+        return stream_part(k, at(k * PIECE, PIECE))
+
+    small_copies = [stream_part(big + i, at(*place)) for i, place in enumerate(small)]
 
     def mate_copy(k):
-        return send(frames_ref.at[0, :, at(k)], ab.at[mate_rows, at(k)], (mate_send.at[k], mate_recv.at[k]), mate, x)
+        columns = at(k * PIECE, PIECE)
+        return send(frames_ref.at[0, :, columns], ab.at[mate_rows, columns], (mate_send.at[k], mate_recv.at[k]), mate, x)
 
     own_copy = pltpu.make_async_copy(frames_ref.at[0], ab.at[own_rows], own_sem.at[0])
     label_copy = pltpu.make_async_copy(label_ref, label, own_sem.at[1])
+    lag_copy = pltpu.make_async_copy(lag_ref, widths, own_sem.at[2])
 
     def early(i):
         return early_send.at[i], early_recv.at[i]
@@ -140,30 +157,32 @@
             device_id_type=MESH,
         )
 
-    own_copy.start()
-    label_copy.start()
     barrier = pltpu.get_barrier_semaphore()
     for tm, pix in ((ahead, x), (behind, x), (mate, x), (me, other)):
         pl.semaphore_signal(barrier, inc=1, device_id={"tm": tm, "pix": pix}, device_id_type=MESH)
     pl.semaphore_wait(barrier, 4)
 
-    @pl.loop(0, chunks)
+    @pl.loop(0, held)
     def _(k):
         stream_copy(k).start()
 
+    label_copy.start()
+    own_copy.start()
+    lag_copy.start()
+
     @pl.when(odd == 1)
     def _():
-        @pl.loop(0, chunks)
+        @pl.loop(0, big + 1)
         def _(k):
             mate_copy(k).start()
 
     for tm, pix in ((mate, x), (me, other)):
         pl.semaphore_signal(extended, inc=1, device_id={"tm": tm, "pix": pix}, device_id_type=MESH)
 
-    label_copy.wait()
     acc1[...] = jnp.zeros_like(acc1)
     acc2[...] = jnp.zeros_like(acc2)
     ab[0:ONES, :] = jnp.ones((ONES, pixels), jnp.bfloat16)
+    label_copy.wait()
 
     @pl.loop(0, chunks)
     def _(k):
@@ -182,32 +201,17 @@
 
     @pl.when(even)
     def _():
-        @pl.loop(0, chunks)
-        def _(k):
-            mate_copy(k).wait_recv()
-            masks = mask[:, :, at(k)]
-            acc1[1] += contract(ab[0 : ONES + f, at(k)], over_rows(masks, ab[mate_rows, at(k)]))
+        @pl.loop(0, big + 1)
+        def _(piece):
+            mate_copy(piece).wait_recv()
+
+            @pl.loop(piece * PIECE, piece * PIECE + PIECE)
+            def _(k):
+                masks = mask[:, :, at(k)]
+                acc1[1] += contract(ab[0 : ONES + f, at(k)], over_rows(masks, ab[mate_rows, at(k)]))
 
         pix_copies[1].start()
 
-    def streamed(start, stop):
-        @pl.when(even)
-        def _():
-            @pl.loop(start, stop)
-            def _(k):
-                stream_copy(k).wait_recv()
-                columns = over_rows(mask[:, :, at(k)], stream[:, at(k)])
-                acc2[...] += contract(ab[ONES : ONES + 2 * f, at(k)], columns)
-
-        @pl.when(odd == 1)
-        def _():
-            @pl.loop(start, stop)
-            def _(k):
-                stream_copy(k).wait_recv()
-                columns = over_rows(mask[:, :, at(k)], ab[own_rows, at(k)])
-                acc2[0:f] += contract(stream[:, at(k)], columns)
-
-    streamed(0, chunks // 4)
     pix_copies[0].wait()
     sums[0] = acc1[0, 0:8] + from_pix[0, 0:8]
     sums_back.start()
@@ -216,24 +220,46 @@
     def _():
         sums_mate_odd.start()
 
-    streamed(chunks // 4, chunks // 2)
+    @pl.loop(held, big)
+    def _(k):
+        stream_copy(k).start()
+
+    for copy in small_copies:
+        copy.start()
+
+    def multiplied(start, stop):
+        @pl.when(even)
+        def _():
+            @pl.loop(start, stop)
+            def _(k):
+                columns = over_rows(mask[:, :, at(k)], stream[:, at(k)])
+                acc2[...] += contract(ab[ONES : ONES + 2 * f, at(k)], columns)
+
+        @pl.when(odd == 1)
+        def _():
+            @pl.loop(start, stop)
+            def _(k):
+                columns = over_rows(mask[:, :, at(k)], ab[own_rows, at(k)])
+                acc2[0:f] += contract(stream[:, at(k)], columns)
+
+    @pl.loop(0, held)
+    def _(piece):
+        stream_copy(piece).wait_recv()
+        multiplied(piece * PIECE, piece * PIECE + PIECE)
+
     sums_back.wait()
 
     @pl.when(even)
     def _():
         sums_mate_even.start()
         pix_copies[1].wait()
-
-    streamed(chunks // 2, 3 * chunks // 4)
-
-    @pl.when(even)
-    def _():
         sums_mate_even.wait()
 
     @pl.when(odd == 1)
     def _():
         sums_mate_odd.wait()
 
+    lag_copy.wait()
     row = lax.broadcasted_iota(jnp.int32, (f, 2 * f), 0)
     lane = lax.broadcasted_iota(jnp.int32, (f, 2 * f), 1)
     lag = x * f + lane
@@ -243,7 +269,7 @@
         own = joined(sums[0], sums[0], a)[0:1]
         own = jnp.sum(jnp.where(row == lane, jnp.broadcast_to(own, (f, 2 * f)), 0.0), axis=1, keepdims=True)
         there = skewed(jnp.broadcast_to(joined(near, far, a)[0:1], (f, 2 * f)))
-        valid = (lag < lag_ref[0, a]) & inside
+        valid = (lag < widths[0, a]) & inside
         weight[a] = jnp.where(valid, annulus_size / (own * there), 0.0)
 
     @pl.when(even & (x == 0))
@@ -260,7 +286,15 @@
         left[...] = acc1[0, own_rows] + from_pix[0, own_rows]
 
     pl.semaphore_wait(extended, 2)
-    streamed(3 * chunks // 4, chunks)
+
+    @pl.loop(held, big)
+    def _(piece):
+        stream_copy(piece).wait_recv()
+        multiplied(piece * PIECE, piece * PIECE + PIECE)
+
+    for copy, (first, count) in zip(small_copies, small):
+        copy.wait_recv()
+        multiplied(first, first + count)
 
     @pl.when(even)
     def _():
@@ -296,13 +330,16 @@
     for a in range(RADII):
         out_ref[0, a] = (skewed(joined(left[...], right[...], a)) * weight[a])[:, 0:f]
 
-    @pl.loop(0, chunks)
+    @pl.loop(0, big)
     def _(k):
         stream_copy(k).wait_send()
 
+    for copy in small_copies:
+        copy.wait_send()
+
     @pl.when(odd == 1)
     def _():
-        @pl.loop(0, chunks)
+        @pl.loop(0, big + 1)
         def _(k):
             mate_copy(k).wait_send()
 
@@ -323,15 +360,16 @@
 
     def shards(frames, annulus_label, lag_width):
         _, f, pixels = frames.shape
-        chunks = pixels // min(CHUNK, pixels // 4)
+        _, big, small = pieces_of(pixels)
+        parts = big + len(small)
         annulus_size = pixels * mesh.shape["pix"] // RADII
         width = RADII * f
         any_space = pl.BlockSpec(memory_space=pl.ANY)
         dma = pltpu.SemaphoreType.DMA
         return pl.pallas_call(
             functools.partial(kernel, n, float(annulus_size)),
-            out_shape=jax.ShapeDtypeStruct((1, RADII, f, f), jnp.float32),
-            in_specs=[any_space, any_space, pl.BlockSpec(memory_space=pltpu.SMEM)],
+            out_shape=pltpu.VMEM((1, RADII, f, f), jnp.float32),
+            in_specs=[any_space] * 3,
             out_specs=pl.BlockSpec(memory_space=pltpu.VMEM),
             scratch_shapes=[
                 pltpu.VMEM((ONES + 2 * f, pixels), jnp.bfloat16),
@@ -348,11 +386,12 @@
                 pltpu.VMEM((f, width), jnp.float32),
                 pltpu.VMEM((f, width), jnp.float32),
                 pltpu.VMEM((RADII, f, 2 * f), jnp.float32),
-                dma((2,)),
-                dma((chunks,)),
-                dma((chunks,)),
-                dma((chunks,)),
-                dma((chunks,)),
+                pltpu.SMEM((1, RADII), jnp.int32),
+                dma((3,)),
+                dma((parts,)),
+                dma((parts,)),
+                dma((big + 1,)),
+                dma((big + 1,)),
                 dma((4,)),
                 dma((4,)),
                 dma((4,)),

time: 69.9 us -> 59.6 us (0.85)
  Pallas kernels: 68.2 us -> 58.3 us
  local copies, waits for them, and re-layouts: 1.57 us -> 0.66 us
    pallas_call x1, Pallas kernels: 68.2 us -> 58.3 us  [shards(): pl.pallas_call(functools.partial(kernel, n, float(annulus_size)), out_sha...]
    unnamed x1, local copies, waits for them, and re-layouts: 1.57 us -> 0.66 us
where the time goes in v2:
time: 59.6 us; the launch traced here: 59 us
  Pallas kernels  58.3 us (98%)
  local copies, waits for them, and re-layouts  0.66 us (1%)
    pallas_call x1, Pallas kernels, shards(): pl.pallas_call(functools.partial(kernel, n, float(annulus_size)), out_sha...  58.3 us

profile of v2, /device:TPU:1, one launch (start us, length us, event | category | flops | bytes accessed | tf_op | source)
XLA Modules:
  0.0 59.0 jit_solution(8833637475830407014)
XLA Ops:
  0.0 58.3 %two_time.1 = f32[1,4,64,64]{3,2,1,0:T(8,128)S(1)} custom-call(bf16[1,64,32768]{2,1,0:T(8,128)(2,1)} %frames_ref.1, s32[1,32768]{1,0:T(1,128)} %label_ref.1, s32[1,4]{1,0:T(1,128)} %lag_ref.1), custom_call_target="tpu_custom_call" | custom-call | tf_op jit(solution)/shard_map/two_time/pallas_call | solution.py:369
  58.3 0.7 %copy.5 = f32[1,4,64,64]{3,2,1,0:T(8,128)} copy(f32[1,4,64,64]{3,2,1,0:T(8,128)S(1)} %two_time.1) | data formatting | bytes 131072

commit v3 on v2

--- a/solution.py
+++ b/solution.py
@@ -10,46 +10,50 @@
 MESH = pl.DeviceIdType.MESH
 RADII = 4
 CHUNK = 1024
-PIECE = 4
+PIECE = 8
 ONES = 16
 
 
 def pieces_of(pixels):
-    chunk = min(CHUNK, pixels // 16)
-    big = pixels // (chunk * PIECE) - 1
-    first = big * PIECE
-    return chunk, big, ((first, 2), (first + 2, 1), (first + 3, 1))
+    chunk = min(CHUNK, pixels // 32)
+    piece = chunk * PIECE
+    big = pixels // piece - 1
+    first = big * piece
+    small = ((first, piece // 2), (first + piece // 2, piece // 4), (first + piece * 3 // 4, piece // 8))
+    return chunk, big, small + ((first + piece * 7 // 8, piece // 16), (first + piece * 15 // 16, piece // 16))
 
 
 def over_rows(masks, block):
-    groups = block.reshape(1, -1, 16, block.shape[-1])
-    return (groups * masks[:, None]).reshape(-1, block.shape[-1])
+    groups = block.reshape(2, 1, -1, 16, block.shape[-1])
+    return (groups * masks[None, :, None]).reshape(-1, block.shape[-1])
 
 
 def contract(rows, columns):
     return lax.dot_general(rows, columns, (((1,), (1,)), ((), ())), preferred_element_type=jnp.float32)
 
 
-def skewed(tile):
-    rows, width = tile.shape
-    groups = [pltpu.roll(tile[g : g + 8], (width - g) % width, 1) for g in range(0, rows, 8)]
-    tile = jnp.concatenate(groups, axis=0)
-    row = lax.broadcasted_iota(jnp.int32, tile.shape, 0)
-    for step in (1, 2, 4):
-        tile = jnp.where(row & step != 0, pltpu.roll(tile, width - step, 1), tile)
-    return tile
-
-
-def joined(left, right, radius):
-    width = left.shape[1] // RADII
-    lanes = slice(radius // 2 * 2 * width, (radius // 2 + 1) * 2 * width)
-    left, right = left[:, lanes], right[:, lanes]
-    if radius % 2:
-        left = pltpu.roll(left, width, 1)
-    else:
-        right = pltpu.roll(right, width, 1)
-    lane = lax.broadcasted_iota(jnp.int32, left.shape, 1)
-    return jnp.where(lane < width, left, right)
+def joined(left, right, radius, skew):
+    width = left.shape[1] // 2
+    quarter = width // RADII
+    shape = (left.shape[0], width)
+    place = lax.broadcasted_iota(jnp.int32, shape, 1)
+    if skew:
+        place = (place + lax.broadcasted_iota(jnp.int32, shape, 0)) & (width - 1)
+    result = None
+    for i in range(4):
+        piece = (left, right)[i // 2][:, i % 2 * width : (i % 2 + 1) * width]
+        lanes = (place + (radius - i) % 4 * quarter) & (width - 1)
+        piece = jnp.take_along_axis(piece, lanes, axis=1)
+        result = piece if result is None else jnp.where(place < i * quarter, result, piece)
+    return result
+
+
+def halves(f, below):
+    lanes = RADII * f // 2
+    first, second = slice(0, lanes), slice(lanes, 2 * lanes)
+    if below:
+        return ((0, f, first), (f // 2, f, second))
+    return ((0, f, second), (0, f // 2, first))
 
 
 def kernel(
@@ -84,11 +88,12 @@
     late_send,
     late_recv,
     extended,
+    known,
 ):
     f, pixels = frames_ref.shape[1:]
     chunk, big, small = pieces_of(pixels)
     chunks = pixels // chunk
-    held = big * 5 // 7
+    held = 2
     own_rows, mate_rows = slice(ONES, ONES + f), slice(ONES + f, ONES + 2 * f)
 
     me, x = lax.axis_index("tm"), lax.axis_index("pix")
@@ -97,6 +102,10 @@
     mate = me + 1 - 2 * odd
     ahead, behind = lax.rem(me + 2, n), lax.rem(me + n - 2, n)
     target = lax.rem(me + n - 2 + 4 * odd, n)
+    source = lax.rem(me + n + 2 - 4 * odd, n)
+    has_behind, has_ahead = me >= 2, me < n - 2
+    sends = (even & has_behind) | ((odd == 1) & has_ahead)
+    receives = (even & has_ahead) | ((odd == 1) & has_behind)
     other = 1 - x
 
     def at(k, count=1):
@@ -115,7 +124,7 @@
     def stream_copy(k):
         return stream_part(k, at(k * PIECE, PIECE))
 
-    small_copies = [stream_part(big + i, at(*place)) for i, place in enumerate(small)]
+    small_copies = [stream_part(big + i, pl.ds(*place)) for i, place in enumerate(small)]
 
     def mate_copy(k):
         columns = at(k * PIECE, PIECE)
@@ -135,49 +144,68 @@
     sums_back = send(sums.at[0], sums.at[2], early(2), behind, x)
     sums_mate_odd = send(sums.at[0], sums.at[1], early(3), mate, x)
     sums_mate_even = send(sums.at[2], sums.at[1], early(3), mate, x)
-    ac_copy = send(acc2.at[0:f], from_even_x0, late(0), me, other)
-
-    def bc_copy(x_from, x_to, way):
-        return pltpu.make_async_remote_copy(
-            src_ref=acc2.at[f : 2 * f],
-            dst_ref=from_even.at[x_from],
-            send_sem=late_send.at[way],
-            recv_sem=late_recv.at[x_from + 1],
-            device_id={"tm": mate, "pix": x_to},
-            device_id_type=MESH,
-        )
-
-    def bd_copy(x_from):
-        return pltpu.make_async_remote_copy(
-            src_ref=acc2.at[0:f],
-            dst_ref=from_next.at[x_from],
-            send_sem=late_send.at[3],
-            recv_sem=late_recv.at[3 + x_from],
-            device_id={"tm": behind, "pix": 1},
-            device_id_type=MESH,
-        )
-
-    barrier = pltpu.get_barrier_semaphore()
-    for tm, pix in ((ahead, x), (behind, x), (mate, x), (me, other)):
-        pl.semaphore_signal(barrier, inc=1, device_id={"tm": tm, "pix": pix}, device_id_type=MESH)
-    pl.semaphore_wait(barrier, 4)
-
-    @pl.loop(0, held)
-    def _(k):
-        stream_copy(k).start()
+    def late_copies(base, dst, below, way, arrival, tm, pix):
+        return [
+            send(
+                acc2.at[base + start : base + stop, lanes],
+                dst.at[start:stop, lanes],
+                (late_send.at[way + i], late_recv.at[arrival + i]),
+                tm,
+                pix,
+            )
+            for i, (start, stop, lanes) in enumerate(halves(f, below))
+        ]
+
+    ac_copies = late_copies(0, from_even_x0, True, 0, 0, me, 1)
+    bc_copies = [
+        [late_copies(f, from_even.at[i], j == 0, 2 + 2 * j, 2 + 2 * i, mate, j) for j in range(2)] for i in range(2)
+    ]
+
+    def bd_copies(x_from):
+        return late_copies(0, from_next.at[x_from], True, 0, 6 + 2 * x_from, behind, 1)
+
+    def each(copies, action):
+        for copy in copies:
+            getattr(copy, action)()
+
+    def signal(semaphore, tm, pix):
+        pl.semaphore_signal(semaphore, inc=1, device_id={"tm": tm, "pix": pix}, device_id_type=MESH)
+
+    def one_if(condition):
+        return jnp.where(condition, 1, 0).astype(jnp.int32)
 
     label_copy.start()
     own_copy.start()
     lag_copy.start()
 
+    barrier = pltpu.get_barrier_semaphore()
+
+    @pl.when(receives)
+    def _():
+        signal(barrier, source, x)
+
+    signal(barrier, mate, x)
+    signal(barrier, me, other)
+    pl.semaphore_wait(barrier, 2 + one_if(sends))
+
+    @pl.when(sends)
+    def _():
+        @pl.loop(0, held)
+        def _(k):
+            stream_copy(k).start()
+
+        signal(known, target, x)
+
     @pl.when(odd == 1)
     def _():
         @pl.loop(0, big + 1)
         def _(k):
             mate_copy(k).start()
 
-    for tm, pix in ((mate, x), (me, other)):
-        pl.semaphore_signal(extended, inc=1, device_id={"tm": tm, "pix": pix}, device_id_type=MESH)
+    @pl.when(~has_ahead)
+    def _():
+        sums[2] = jnp.zeros_like(sums[2])
+        from_next[...] = jnp.zeros_like(from_next)
 
     acc1[...] = jnp.zeros_like(acc1)
     acc2[...] = jnp.zeros_like(acc2)
@@ -199,6 +227,13 @@
 
     pix_copies[0].start()
 
+    @pl.when(receives)
+    def _():
+        pl.semaphore_wait(known, 1)
+
+    signal(extended, mate, x)
+    signal(extended, me, other)
+
     @pl.when(even)
     def _():
         @pl.loop(0, big + 1)
@@ -214,40 +249,53 @@
 
     pix_copies[0].wait()
     sums[0] = acc1[0, 0:8] + from_pix[0, 0:8]
-    sums_back.start()
+
+    @pl.when(has_behind)
+    def _():
+        sums_back.start()
 
     @pl.when(odd == 1)
     def _():
         sums_mate_odd.start()
 
-    @pl.loop(held, big)
-    def _(k):
-        stream_copy(k).start()
-
-    for copy in small_copies:
-        copy.start()
-
-    def multiplied(start, stop):
+    @pl.when(sends)
+    def _():
+        @pl.loop(held, big)
+        def _(k):
+            stream_copy(k).start()
+
+        for copy in small_copies:
+            copy.start()
+
+    def multiply(columns):
         @pl.when(even)
         def _():
-            @pl.loop(start, stop)
-            def _(k):
-                columns = over_rows(mask[:, :, at(k)], stream[:, at(k)])
-                acc2[...] += contract(ab[ONES : ONES + 2 * f, at(k)], columns)
+            spread = over_rows(mask[:, :, columns], stream[:, columns])
+            acc2[...] += contract(ab[ONES : ONES + 2 * f, columns], spread)
 
         @pl.when(odd == 1)
         def _():
-            @pl.loop(start, stop)
-            def _(k):
-                columns = over_rows(mask[:, :, at(k)], ab[own_rows, at(k)])
-                acc2[0:f] += contract(stream[:, at(k)], columns)
-
-    @pl.loop(0, held)
-    def _(piece):
+            spread = over_rows(mask[:, :, columns], ab[own_rows, columns])
+            acc2[0:f] += contract(stream[:, columns], spread)
+
+    def multiply_piece(piece):
         stream_copy(piece).wait_recv()
-        multiplied(piece * PIECE, piece * PIECE + PIECE)
-
-    sums_back.wait()
+
+        @pl.loop(piece * PIECE, piece * PIECE + PIECE)
+        def _(k):
+            multiply(at(k))
+
+    @pl.when(receives)
+    def _():
+        pl.loop(0, held)(multiply_piece)
+
+    @pl.when(has_ahead)
+    def _():
+        sums_back.wait_recv()
+
+    @pl.when(has_behind)
+    def _():
+        sums_back.wait_send()
 
     @pl.when(even)
     def _():
@@ -264,11 +312,12 @@
     lane = lax.broadcasted_iota(jnp.int32, (f, 2 * f), 1)
     lag = x * f + lane
     inside = me * f + row + lag < n * f
-    near, far = sums[x], sums[x + 1]
+    near, far = sums[x, 0:1], sums[x + 1, 0:1]
+    wide = (f, RADII * f)
     for a in range(RADII):
-        own = joined(sums[0], sums[0], a)[0:1]
+        own = joined(sums[0], sums[0], a, False)[0:1]
         own = jnp.sum(jnp.where(row == lane, jnp.broadcast_to(own, (f, 2 * f)), 0.0), axis=1, keepdims=True)
-        there = skewed(jnp.broadcast_to(joined(near, far, a)[0:1], (f, 2 * f)))
+        there = joined(jnp.broadcast_to(near, wide), jnp.broadcast_to(far, wide), a, True)
         valid = (lag < widths[0, a]) & inside
         weight[a] = jnp.where(valid, annulus_size / (own * there), 0.0)
 
@@ -287,55 +336,66 @@
 
     pl.semaphore_wait(extended, 2)
 
-    @pl.loop(held, big)
-    def _(piece):
-        stream_copy(piece).wait_recv()
-        multiplied(piece * PIECE, piece * PIECE + PIECE)
-
-    for copy, (first, count) in zip(small_copies, small):
-        copy.wait_recv()
-        multiplied(first, first + count)
+    @pl.when(receives)
+    def _():
+        pl.loop(held, big)(multiply_piece)
+
+        for copy, (first, count) in zip(small_copies, small):
+            copy.wait_recv()
+            step = min(chunk, count)
+
+            @pl.loop(0, count // step)
+            def _(k, first=first, step=step):
+                multiply(pl.ds(pl.multiple_of(first + k * step, step), step))
 
     @pl.when(even)
     def _():
         @pl.when(x == 0)
         def _():
-            ac_copy.start()
-
-        bc_copy(x, other, 1).start()
-        bc_copy(x, x, 2).start()
+            each(bc_copies[0][1], "start")
+            each(ac_copies, "start")
+            each(bc_copies[0][0], "start")
 
         @pl.when(x == 1)
         def _():
-            ac_copy.wait_recv()
+            each(bc_copies[1][0], "start")
+            each(bc_copies[1][1], "start")
+            each(ac_copies, "wait_recv")
             right[...] = acc2[0:f] + from_even_x0[...]
 
     @pl.when(odd == 1)
     def _():
-        bd_copy(x).start()
-        bc_copy(0, 0, 1).wait_recv()
-        bc_copy(1, 0, 1).wait_recv()
+        @pl.when(has_behind)
+        def _():
+            each(bd_copies(x), "start")
 
         @pl.when(x == 0)
         def _():
+            each(bc_copies[0][0] + bc_copies[1][0], "wait_recv")
             right[...] = from_even[0] + from_even[1]
 
         @pl.when(x == 1)
         def _():
+            each(bc_copies[0][1] + bc_copies[1][1], "wait_recv")
             left[...] = from_even[0] + from_even[1]
-            bd_copy(0).wait_recv()
-            bd_copy(1).wait_recv()
+
+            @pl.when(has_ahead)
+            def _():
+                each(bd_copies(0) + bd_copies(1), "wait_recv")
+
             right[...] = from_next[0] + from_next[1]
 
     for a in range(RADII):
-        out_ref[0, a] = (skewed(joined(left[...], right[...], a)) * weight[a])[:, 0:f]
-
-    @pl.loop(0, big)
-    def _(k):
-        stream_copy(k).wait_send()
-
-    for copy in small_copies:
-        copy.wait_send()
+        out_ref[0, a] = (joined(left[...], right[...], a, True) * weight[a])[:, 0:f]
+
+    @pl.when(sends)
+    def _():
+        @pl.loop(0, big)
+        def _(k):
+            stream_copy(k).wait_send()
+
+        for copy in small_copies:
+            copy.wait_send()
 
     @pl.when(odd == 1)
     def _():
@@ -343,16 +403,21 @@
         def _(k):
             mate_copy(k).wait_send()
 
-        bd_copy(x).wait_send()
+        @pl.when(has_behind)
+        def _():
+            each(bd_copies(x), "wait_send")
 
     @pl.when(even)
     def _():
+        for i in range(2):
+
+            @pl.when(x == i)
+            def _(i=i):
+                each(bc_copies[i][0] + bc_copies[i][1], "wait_send")
+
         @pl.when(x == 0)
         def _():
-            ac_copy.wait_send()
-
-        bc_copy(x, other, 1).wait_send()
-        bc_copy(x, x, 2).wait_send()
+            each(ac_copies, "wait_send")
 
 
 def solution(mesh):
@@ -394,8 +459,9 @@
                 dma((big + 1,)),
                 dma((4,)),
                 dma((4,)),
-                dma((4,)),
-                dma((5,)),
+                dma((6,)),
+                dma((10,)),
+                pltpu.SemaphoreType.REGULAR,
                 pltpu.SemaphoreType.REGULAR,
             ],
             compiler_params=pltpu.CompilerParams(collective_id=0, has_side_effects=True),

time: 59.6 us -> 56.5 us (0.948)
  Pallas kernels: 58.3 us -> 54.9 us
    pallas_call x1, Pallas kernels: 58.3 us -> 54.9 us  [shards(): pl.pallas_call(functools.partial(kernel, n, float(annulus_size)), out_sha...]
where the time goes in v3:
time: 56.5 us; the launch traced here: 55.6 us
  Pallas kernels  54.9 us (97%)
  local copies, waits for them, and re-layouts  0.66 us (1%)
    pallas_call x1, Pallas kernels, shards(): pl.pallas_call(functools.partial(kernel, n, float(annulus_size)), out_sha...  54.9 us

profile of v3, /device:TPU:1, one launch (start us, length us, event | category | flops | bytes accessed | tf_op | source)
XLA Modules:
  0.0 55.6 jit_solution(6955649558963971295)
XLA Ops:
  0.0 54.9 %two_time.1 = f32[1,4,64,64]{3,2,1,0:T(8,128)S(1)} custom-call(bf16[1,64,32768]{2,1,0:T(8,128)(2,1)} %frames_ref.1, s32[1,32768]{1,0:T(1,128)} %label_ref.1, s32[1,4]{1,0:T(1,128)} %lag_ref.1), custom_call_target="tpu_custom_call" | custom-call | tf_op jit(solution)/shard_map/two_time/pallas_call | solution.py:434
  54.9 0.7 %copy.5 = f32[1,4,64,64]{3,2,1,0:T(8,128)} copy(f32[1,4,64,64]{3,2,1,0:T(8,128)S(1)} %two_time.1) | data formatting | bytes 131072

commit v4 on v3

--- a/solution.py
+++ b/solution.py
@@ -10,17 +10,22 @@
 MESH = pl.DeviceIdType.MESH
 RADII = 4
 CHUNK = 1024
-PIECE = 8
+MATE_PIECES = 4
 ONES = 16
 
 
 def pieces_of(pixels):
-    chunk = min(CHUNK, pixels // 32)
-    piece = chunk * PIECE
-    big = pixels // piece - 1
-    first = big * piece
-    small = ((first, piece // 2), (first + piece // 2, piece // 4), (first + piece * 3 // 4, piece // 8))
-    return chunk, big, small + ((first + piece * 7 // 8, piece // 16), (first + piece * 15 // 16, piece // 16))
+    late, first, width = [], 0, pixels // 2
+    while width >= pixels // 64:
+        late.append((1, first, width))
+        first, width = first + width, width // 2
+    early = [(0, 0, pixels)]
+    return early, late + [(1, first, pixels - first)]
+
+
+def over_half(masks, rows):
+    groups = rows.reshape(1, -1, 16, rows.shape[-1])
+    return (groups * masks[:, None]).reshape(-1, rows.shape[-1])
 
 
 def over_rows(masks, block):
@@ -48,12 +53,10 @@
     return result
 
 
-def halves(f, below):
-    lanes = RADII * f // 2
-    first, second = slice(0, lanes), slice(lanes, 2 * lanes)
+def needed(f, half, below):
     if below:
-        return ((0, f, first), (f // 2, f, second))
-    return ((0, f, second), (0, f // 2, first))
+        return (0, f) if half == 0 else (f // 2, f)
+    return (0, f // 2) if half == 0 else (0, f)
 
 
 def kernel(
@@ -71,9 +74,12 @@
     acc2,
     from_pix,
     sums,
+    low,
+    high,
     from_even,
     from_even_x0,
-    from_next,
+    from_next_low,
+    from_next_high,
     left,
     right,
     weight,
@@ -91,9 +97,11 @@
     known,
 ):
     f, pixels = frames_ref.shape[1:]
-    chunk, big, small = pieces_of(pixels)
-    chunks = pixels // chunk
-    held = 2
+    early_pieces, late_pieces = pieces_of(pixels)
+    chunk = min(CHUNK, pixels // 32)
+    chunks, per_piece = pixels // chunk, pixels // chunk // MATE_PIECES
+    h = f // 2
+    tiles = (slice(0, RADII * h), slice(RADII * h, RADII * f))
     own_rows, mate_rows = slice(ONES, ONES + f), slice(ONES + f, ONES + 2 * f)
 
     me, x = lax.axis_index("tm"), lax.axis_index("pix")
@@ -116,18 +124,20 @@
             src_ref=src, dst_ref=dst, send_sem=sems[0], recv_sem=sems[1], device_id={"tm": tm, "pix": pix}, device_id_type=MESH
         )
 
-    def stream_part(i, columns):
-        return send(
-            frames_ref.at[0, :, columns], stream.at[:, columns], (stream_send.at[i], stream_recv.at[i]), target, x
+    stream_copies = [
+        send(
+            frames_ref.at[0, half * h : (half + 1) * h, pl.ds(first, width)],
+            stream.at[half * h : (half + 1) * h, pl.ds(first, width)],
+            (stream_send.at[i], stream_recv.at[i]),
+            target,
+            x,
         )
-
-    def stream_copy(k):
-        return stream_part(k, at(k * PIECE, PIECE))
-
-    small_copies = [stream_part(big + i, pl.ds(*place)) for i, place in enumerate(small)]
+        for i, (half, first, width) in enumerate(early_pieces + late_pieces)
+    ]
+    early_copies, late_copies = stream_copies[: len(early_pieces)], stream_copies[len(early_pieces) :]
 
     def mate_copy(k):
-        columns = at(k * PIECE, PIECE)
+        columns = at(k * per_piece, per_piece)
         return send(frames_ref.at[0, :, columns], ab.at[mate_rows, columns], (mate_send.at[k], mate_recv.at[k]), mate, x)
 
     own_copy = pltpu.make_async_copy(frames_ref.at[0], ab.at[own_rows], own_sem.at[0])
@@ -144,25 +154,66 @@
     sums_back = send(sums.at[0], sums.at[2], early(2), behind, x)
     sums_mate_odd = send(sums.at[0], sums.at[1], early(3), mate, x)
     sums_mate_even = send(sums.at[2], sums.at[1], early(3), mate, x)
-    def late_copies(base, dst, below, way, arrival, tm, pix):
+    def tile_copies(base, dst, below, way, arrival, tm, pix):
+        copies = []
+        for half in range(2):
+            start, stop = needed(f, half, below)
+            src = acc2.at[half, base + start : base + stop]
+            sems = (late_send.at[way + half], late_recv.at[arrival + half])
+            copies.append(send(src, dst.at[half, start:stop], sems, tm, pix))
+        return copies
+
+    ac_copies = tile_copies(0, from_even_x0, True, 0, 0, me, 1)
+    bc_copies = [
+        [tile_copies(f, from_even.at[i], j == 0, 2 + 2 * j, 2 + 2 * i, mate, j) for j in range(2)] for i in range(2)
+    ]
+
+    def bd_copies(x_from):
         return [
-            send(
-                acc2.at[base + start : base + stop, lanes],
-                dst.at[start:stop, lanes],
-                (late_send.at[way + i], late_recv.at[arrival + i]),
-                tm,
-                pix,
-            )
-            for i, (start, stop, lanes) in enumerate(halves(f, below))
+            send(src, dst.at[x_from], (late_send.at[i], late_recv.at[6 + 2 * x_from + i]), behind, 1)
+            for i, (src, dst) in enumerate(((low, from_next_low), (high, from_next_high)))
         ]
 
-    ac_copies = late_copies(0, from_even_x0, True, 0, 0, me, 1)
-    bc_copies = [
-        [late_copies(f, from_even.at[i], j == 0, 2 + 2 * j, 2 + 2 * i, mate, j) for j in range(2)] for i in range(2)
-    ]
-
-    def bd_copies(x_from):
-        return late_copies(0, from_next.at[x_from], True, 0, 6 + 2 * x_from, behind, 1)
+    def exchange(half):
+        @pl.when(even & (x == 0))
+        def _():
+            each([ac_copies[half], bc_copies[0][1][half], bc_copies[0][0][half]], "start")
+
+        @pl.when(even & (x == 1))
+        def _():
+            each([bc_copies[1][0][half], bc_copies[1][1][half]], "start")
+
+        if half == 1:
+
+            @pl.when((odd == 1) & has_behind)
+            def _():
+                each(bd_copies(x)[::-1], "start")
+
+    def gather(half):
+        below, above = slice(*needed(f, half, True)), slice(*needed(f, half, False))
+
+        @pl.when(even & (x == 1))
+        def _():
+            ac_copies[half].wait_recv()
+            right[below, tiles[half]] = acc2[half, below] + from_even_x0[half, below]
+
+        @pl.when((odd == 1) & (x == 0))
+        def _():
+            each([bc_copies[0][0][half], bc_copies[1][0][half]], "wait_recv")
+            right[below, tiles[half]] = from_even[0, half, below] + from_even[1, half, below]
+
+        @pl.when((odd == 1) & (x == 1))
+        def _():
+            each([bc_copies[0][1][half], bc_copies[1][1][half]], "wait_recv")
+            left[above, tiles[half]] = from_even[0, half, above] + from_even[1, half, above]
+
+        if half == 1:
+
+            @pl.when((odd == 1) & (x == 1) & has_ahead)
+            def _():
+                each(bd_copies(0) + bd_copies(1), "wait_recv")
+                right[0:h, tiles[0]] = from_next_low[0] + from_next_low[1]
+                right[h:f] = from_next_high[0] + from_next_high[1]
 
     def each(copies, action):
         for copy in copies:
@@ -190,25 +241,23 @@
 
     @pl.when(sends)
     def _():
-        @pl.loop(0, held)
-        def _(k):
-            stream_copy(k).start()
-
+        each(early_copies, "start")
         signal(known, target, x)
 
     @pl.when(odd == 1)
     def _():
-        @pl.loop(0, big + 1)
+        @pl.loop(0, MATE_PIECES)
         def _(k):
             mate_copy(k).start()
 
     @pl.when(~has_ahead)
     def _():
         sums[2] = jnp.zeros_like(sums[2])
-        from_next[...] = jnp.zeros_like(from_next)
 
     acc1[...] = jnp.zeros_like(acc1)
-    acc2[...] = jnp.zeros_like(acc2)
+    for tile in (acc2, low, high, left, right):
+        tile[...] = jnp.zeros_like(tile)
+
     ab[0:ONES, :] = jnp.ones((ONES, pixels), jnp.bfloat16)
     label_copy.wait()
 
@@ -236,11 +285,11 @@
 
     @pl.when(even)
     def _():
-        @pl.loop(0, big + 1)
+        @pl.loop(0, MATE_PIECES)
         def _(piece):
             mate_copy(piece).wait_recv()
 
-            @pl.loop(piece * PIECE, piece * PIECE + PIECE)
+            @pl.loop(piece * per_piece, piece * per_piece + per_piece)
             def _(k):
                 masks = mask[:, :, at(k)]
                 acc1[1] += contract(ab[0 : ONES + f, at(k)], over_rows(masks, ab[mate_rows, at(k)]))
@@ -260,34 +309,40 @@
 
     @pl.when(sends)
     def _():
-        @pl.loop(held, big)
-        def _(k):
-            stream_copy(k).start()
-
-        for copy in small_copies:
-            copy.start()
-
-    def multiply(columns):
+        each(late_copies, "start")
+
+    def multiply(half, columns):
+        rows = slice(half * h, (half + 1) * h)
+
         @pl.when(even)
         def _():
-            spread = over_rows(mask[:, :, columns], stream[:, columns])
-            acc2[...] += contract(ab[ONES : ONES + 2 * f, columns], spread)
+            spread = over_half(mask[:, :, columns], stream[rows, columns])
+            first = needed(f, half, True)[0]
+            acc2[half, first : 2 * f] += contract(ab[ONES + first : ONES + 2 * f, columns], spread)
 
         @pl.when(odd == 1)
         def _():
-            spread = over_rows(mask[:, :, columns], ab[own_rows, columns])
-            acc2[0:f] += contract(stream[:, columns], spread)
-
-    def multiply_piece(piece):
-        stream_copy(piece).wait_recv()
-
-        @pl.loop(piece * PIECE, piece * PIECE + PIECE)
-        def _(k):
-            multiply(at(k))
-
-    @pl.when(receives)
-    def _():
-        pl.loop(0, held)(multiply_piece)
+            if half == 0:
+                spread = over_half(mask[:, :, columns], ab[ONES : ONES + h, columns])
+                low[...] += contract(stream[rows, columns], spread)
+            else:
+                spread = over_rows(mask[:, :, columns], ab[own_rows, columns])
+                high[...] += contract(stream[rows, columns], spread)
+
+    def multiply_all(copies, pieces):
+        @pl.when(receives)
+        def _():
+            for copy, (half, first, width) in zip(copies, pieces):
+                copy.wait_recv()
+                step = min(chunk, width)
+
+                @pl.loop(0, width // step)
+                def _(k, half=half, first=first, step=step):
+                    multiply(half, pl.ds(pl.multiple_of(first + k * step, step), step))
+
+    multiply_all(early_copies, early_pieces)
+    pl.semaphore_wait(extended, 2)
+    exchange(0)
 
     @pl.when(has_ahead)
     def _():
@@ -334,72 +389,22 @@
     def _():
         left[...] = acc1[0, own_rows] + from_pix[0, own_rows]
 
-    pl.semaphore_wait(extended, 2)
-
-    @pl.when(receives)
-    def _():
-        pl.loop(held, big)(multiply_piece)
-
-        for copy, (first, count) in zip(small_copies, small):
-            copy.wait_recv()
-            step = min(chunk, count)
-
-            @pl.loop(0, count // step)
-            def _(k, first=first, step=step):
-                multiply(pl.ds(pl.multiple_of(first + k * step, step), step))
-
-    @pl.when(even)
-    def _():
-        @pl.when(x == 0)
-        def _():
-            each(bc_copies[0][1], "start")
-            each(ac_copies, "start")
-            each(bc_copies[0][0], "start")
-
-        @pl.when(x == 1)
-        def _():
-            each(bc_copies[1][0], "start")
-            each(bc_copies[1][1], "start")
-            each(ac_copies, "wait_recv")
-            right[...] = acc2[0:f] + from_even_x0[...]
-
-    @pl.when(odd == 1)
-    def _():
-        @pl.when(has_behind)
-        def _():
-            each(bd_copies(x), "start")
-
-        @pl.when(x == 0)
-        def _():
-            each(bc_copies[0][0] + bc_copies[1][0], "wait_recv")
-            right[...] = from_even[0] + from_even[1]
-
-        @pl.when(x == 1)
-        def _():
-            each(bc_copies[0][1] + bc_copies[1][1], "wait_recv")
-            left[...] = from_even[0] + from_even[1]
-
-            @pl.when(has_ahead)
-            def _():
-                each(bd_copies(0) + bd_copies(1), "wait_recv")
-
-            right[...] = from_next[0] + from_next[1]
+    multiply_all(late_copies[:1], late_pieces[:1])
+    gather(0)
+    multiply_all(late_copies[1:], late_pieces[1:])
+    exchange(1)
+    gather(1)
 
     for a in range(RADII):
         out_ref[0, a] = (joined(left[...], right[...], a, True) * weight[a])[:, 0:f]
 
     @pl.when(sends)
     def _():
-        @pl.loop(0, big)
-        def _(k):
-            stream_copy(k).wait_send()
-
-        for copy in small_copies:
-            copy.wait_send()
+        each(stream_copies, "wait_send")
 
     @pl.when(odd == 1)
     def _():
-        @pl.loop(0, big + 1)
+        @pl.loop(0, MATE_PIECES)
         def _(k):
             mate_copy(k).wait_send()
 
@@ -425,8 +430,8 @@
 
     def shards(frames, annulus_label, lag_width):
         _, f, pixels = frames.shape
-        _, big, small = pieces_of(pixels)
-        parts = big + len(small)
+        parts = sum(map(len, pieces_of(pixels)))
+        h = f // 2
         annulus_size = pixels * mesh.shape["pix"] // RADII
         width = RADII * f
         any_space = pl.BlockSpec(memory_space=pl.ANY)
@@ -442,12 +447,15 @@
                 pltpu.VMEM((1, pixels), jnp.int32),
                 pltpu.VMEM((RADII, 16, pixels), jnp.bfloat16),
                 pltpu.VMEM((2, ONES + f, width), jnp.float32),
-                pltpu.VMEM((2 * f, width), jnp.float32),
+                pltpu.VMEM((2, 2 * f, width // 2), jnp.float32),
                 pltpu.VMEM((2, ONES + f, width), jnp.float32),
                 pltpu.VMEM((3, 8, width), jnp.float32),
-                pltpu.VMEM((2, f, width), jnp.float32),
-                pltpu.VMEM((f, width), jnp.float32),
-                pltpu.VMEM((2, f, width), jnp.float32),
+                pltpu.VMEM((h, width // 2), jnp.float32),
+                pltpu.VMEM((h, width), jnp.float32),
+                pltpu.VMEM((2, 2, f, width // 2), jnp.float32),
+                pltpu.VMEM((2, f, width // 2), jnp.float32),
+                pltpu.VMEM((2, h, width // 2), jnp.float32),
+                pltpu.VMEM((2, h, width), jnp.float32),
                 pltpu.VMEM((f, width), jnp.float32),
                 pltpu.VMEM((f, width), jnp.float32),
                 pltpu.VMEM((RADII, f, 2 * f), jnp.float32),
@@ -455,8 +463,8 @@
                 dma((3,)),
                 dma((parts,)),
                 dma((parts,)),
-                dma((big + 1,)),
-                dma((big + 1,)),
+                dma((MATE_PIECES,)),
+                dma((MATE_PIECES,)),
                 dma((4,)),
                 dma((4,)),
                 dma((6,)),

time: 56.5 us -> 56.1 us (level)
  no operation moved by 1% of the time
where the time goes in v4:
time: 56.1 us; the launch traced here: 55.1 us
  Pallas kernels  54.5 us (97%)
  local copies, waits for them, and re-layouts  0.66 us (1%)
    pallas_call x1, Pallas kernels, shards(): pl.pallas_call(functools.partial(kernel, n, float(annulus_size)), out_sha...  54.5 us

profile of v4, /device:TPU:1, one launch (start us, length us, event | category | flops | bytes accessed | tf_op | source)
XLA Modules:
  0.0 55.1 jit_solution(10904852815896472155)
XLA Ops:
  0.0 54.5 %two_time.1 = f32[1,4,64,64]{3,2,1,0:T(8,128)S(1)} custom-call(bf16[1,64,32768]{2,1,0:T(8,128)(2,1)} %frames_ref.1, s32[1,32768]{1,0:T(1,128)} %label_ref.1, s32[1,4]{1,0:T(1,128)} %lag_ref.1), custom_call_target="tpu_custom_call" | custom-call | tf_op jit(solution)/shard_map/two_time/pallas_call | solution.py:439
  54.5 0.7 %copy.5 = f32[1,4,64,64]{3,2,1,0:T(8,128)} copy(f32[1,4,64,64]{3,2,1,0:T(8,128)S(1)} %two_time.1) | data formatting | bytes 131072

commit v5 on v4

--- a/solution.py
+++ b/solution.py
@@ -177,7 +177,7 @@
     def exchange(half):
         @pl.when(even & (x == 0))
         def _():
-            each([ac_copies[half], bc_copies[0][1][half], bc_copies[0][0][half]], "start")
+            each([bc_copies[0][1][half], ac_copies[half], bc_copies[0][0][half]], "start")
 
         @pl.when(even & (x == 1))
         def _():
@@ -391,12 +391,31 @@
 
     multiply_all(late_copies[:1], late_pieces[:1])
     gather(0)
+
+    def finish():
+        for a in range(RADII):
+            out_ref[0, a] = (joined(left[...], right[...], a, True) * weight[a])[:, 0:f]
+
+    @pl.when(even | (x == 0))
+    def _():
+        finish()
+
     multiply_all(late_copies[1:], late_pieces[1:])
     exchange(1)
     gather(1)
 
-    for a in range(RADII):
-        out_ref[0, a] = (joined(left[...], right[...], a, True) * weight[a])[:, 0:f]
+    @pl.when((odd == 1) & (x == 1))
+    def _():
+        finish()
+
+    @pl.when(odd + x == 1)
+    def _():
+        place = lax.broadcasted_iota(jnp.int32, (f, 2 * f), 0) + lax.broadcasted_iota(jnp.int32, (f, 2 * f), 1)
+        last = right[:, tiles[1]]
+        for a in range(RADII):
+            lanes = (place + (a + 1) % 4 * h) & (2 * f - 1)
+            patch = (jnp.take_along_axis(last, lanes, axis=1) * weight[a])[:, 0:f]
+            out_ref[0, a] = jnp.where(place[:, 0:f] < 3 * h, out_ref[0, a], patch)
 
     @pl.when(sends)
     def _():

time: 56.1 us -> 55.8 us (level)
  no operation moved by 1% of the time
where the time goes in v5:
time: 55.8 us; the launch traced here: 54.9 us
  Pallas kernels  54.2 us (97%)
  local copies, waits for them, and re-layouts  0.66 us (1%)
    pallas_call x1, Pallas kernels, shards(): pl.pallas_call(functools.partial(kernel, n, float(annulus_size)), out_sha...  54.2 us

profile of v5, /device:TPU:1, one launch (start us, length us, event | category | flops | bytes accessed | tf_op | source)
XLA Modules:
  0.0 54.9 jit_solution(13515533782230912555)
XLA Ops:
  0.0 54.2 %two_time.1 = f32[1,4,64,64]{3,2,1,0:T(8,128)S(1)} custom-call(bf16[1,64,32768]{2,1,0:T(8,128)(2,1)} %frames_ref.1, s32[1,32768]{1,0:T(1,128)} %label_ref.1, s32[1,4]{1,0:T(1,128)} %lag_ref.1), custom_call_target="tpu_custom_call" | custom-call | tf_op jit(solution)/shard_map/two_time/pallas_call | solution.py:458
  54.2 0.7 %copy.5 = f32[1,4,64,64]{3,2,1,0:T(8,128)} copy(f32[1,4,64,64]{3,2,1,0:T(8,128)S(1)} %two_time.1) | data formatting | bytes 131072

commit v6 on v5

--- a/solution.py
+++ b/solution.py
@@ -177,11 +177,13 @@
     def exchange(half):
         @pl.when(even & (x == 0))
         def _():
-            each([bc_copies[0][1][half], ac_copies[half], bc_copies[0][0][half]], "start")
+            each([bc_copies[0][1][0]] if half == 0 else [], "start")
+            each([ac_copies[half], bc_copies[0][0][half]], "start")
 
         @pl.when(even & (x == 1))
         def _():
-            each([bc_copies[1][0][half], bc_copies[1][1][half]], "start")
+            each([bc_copies[1][0][0]] if half == 0 else [], "start")
+            bc_copies[1][1][half].start()
 
         if half == 1:
 
@@ -400,7 +402,35 @@
     def _():
         finish()
 
-    multiply_all(late_copies[1:], late_pieces[1:])
+    multiply_all(late_copies[1:-1], late_pieces[1:-1])
+    _, final_first, final_width = late_pieces[-1]
+    final = pl.ds(final_first, final_width)
+
+    def multiply_rows(start, stop):
+        @pl.when(receives & even)
+        def _():
+            spread = over_half(mask[:, :, final], stream[h:f, final])
+            acc2[1, start:stop] += contract(ab[ONES + start : ONES + stop, final], spread)
+
+    @pl.when(receives)
+    def _():
+        late_copies[-1].wait_recv()
+
+    @pl.when(receives & (odd == 1))
+    def _():
+        multiply(1, final)
+
+    multiply_rows(f, 2 * f)
+
+    @pl.when(even & (x == 0))
+    def _():
+        bc_copies[0][1][1].start()
+
+    @pl.when(even & (x == 1))
+    def _():
+        bc_copies[1][0][1].start()
+
+    multiply_rows(h, f)
     exchange(1)
     gather(1)
 

time: 55.8 us -> 55.8 us (level)
  no operation moved by 1% of the time
where the time goes in v6:
time: 55.8 us; the launch traced here: 54.9 us
  Pallas kernels  54.2 us (97%)
  local copies, waits for them, and re-layouts  0.66 us (1%)
    pallas_call x1, Pallas kernels, shards(): pl.pallas_call(functools.partial(kernel, n, float(annulus_size)), out_sha...  54.2 us

profile of v6, /device:TPU:1, one launch (start us, length us, event | category | flops | bytes accessed | tf_op | source)
XLA Modules:
  0.0 54.9 jit_solution(487437741683316267)
XLA Ops:
  0.0 54.2 %two_time.1 = f32[1,4,64,64]{3,2,1,0:T(8,128)S(1)} custom-call(bf16[1,64,32768]{2,1,0:T(8,128)(2,1)} %frames_ref.1, s32[1,32768]{1,0:T(1,128)} %label_ref.1, s32[1,4]{1,0:T(1,128)} %lag_ref.1), custom_call_target="tpu_custom_call" | custom-call | tf_op jit(solution)/shard_map/two_time/pallas_call | solution.py:488
  54.2 0.7 %copy.5 = f32[1,4,64,64]{3,2,1,0:T(8,128)} copy(f32[1,4,64,64]{3,2,1,0:T(8,128)S(1)} %two_time.1) | data formatting | bytes 131072
